TPU v7x, 128 devices: a whole 4x4x4 slice. The times are simulated.
128 devices in a mesh: sensor: 16 (over y, z_lo, core), channel: 4 (over x), tm: 2 (over z_hi).
Axes of the slice: x: 4, y: 4, z: 4 (z_hi: 2, z_lo: 2; z = z_hi * 2 + z_lo), core: 2. Of those that a mesh axis runs over, the one named last changes fastest.
Arguments:
- tensor: float32 [12288, 128, 512], P('sensor', 'tm', 'channel'), may hold values from -6 to 6
- core: float32 [64, 64, 32], replicated, may hold values from -0.015625 to 0.015625
- sensor_factor: float32 [12288, 64], P('sensor'), may hold values from -6 to 6
- channel_factor: float32 [512, 64], P('channel'), may hold values from -6 to 6
- time_factor: float32 [128, 32], P('tm'), may hold values from -6 to 6
- neighbour_ids: int32 [96, 4], P('sensor'), may hold values from 0 to 95
- edge_weights: int32 [96, 4, 128, 128], P('sensor'), may hold values from 0 to 3
Outputs:
- core_grad: float32 [64, 64, 32], replicated
- sensor_grad: float32 [12288, 64], P(('sensor', 'channel', 'tm'))
- channel_grad: float32 [512, 64], P('channel')
- time_grad: float32 [128, 32], P('tm')
All inputs are finite; a program needn't handle non-finite values.
Results may differ from a plain program's by a relative error of at most 0.0001.
Values sent between devices are 32-bit elements; how exact they have to be, the bound alone decides.
A program may use at most 192 MiB of HBM per device.

v0:
```python
import math
import jax
import jax.numpy as jnp
from jax import lax
from jax.sharding import PartitionSpec as P

lap_weight = 1.0 / 512.0
highest = lax.Precision.HIGHEST


def pulled_rows(whole_factor, neighbour_ids, weights_float, block):
    whole = whole_factor.reshape(-1, block, whole_factor.shape[-1])
    neighbours = whole[neighbour_ids]
    return jnp.einsum("bnic,bncd->bid", weights_float, neighbours, precision=highest)


def on_device(
    tensor, core, sensor_factor, channel_factor, time_factor, neighbour_ids, edge_weights
):
    sensor_rows, time_rows, chan_rows = tensor.shape
    rank_one, rank_two, rank_three = core.shape
    n_sensor = lax.axis_size("sensor")
    n_channel = lax.axis_size("channel")
    n_time = lax.axis_size("tm")
    total_sensors = sensor_rows * n_sensor
    total_time = time_rows * n_time
    total_chan = chan_rows * n_channel
    core_time = jnp.einsum("rst,kt->rks", core, time_factor, precision=highest)
    core_both = jnp.einsum("rks,js->rkj", core_time, channel_factor, precision=highest)
    core_chan = jnp.einsum("rst,js->rtj", core, channel_factor, precision=highest)
    flat_core = core_both.reshape(rank_one, time_rows * chan_rows)
    residual = jnp.dot(sensor_factor, flat_core, precision=highest) - tensor.reshape(
        sensor_rows, time_rows * chan_rows
    )
    folded = jnp.dot(sensor_factor.T, residual, precision=highest)
    fit_part = jnp.dot(residual, flat_core.T, precision=highest) / math.sqrt(
        total_time * total_chan
    )
    folded3 = folded.reshape(rank_one, time_rows, chan_rows)
    inner = jnp.einsum("rkj,js->rks", folded3, channel_factor, precision=highest)
    core_part = jnp.einsum("rks,kt->rst", inner, time_factor, precision=highest) / math.sqrt(
        total_sensors * total_time * total_chan
    )
    chan_part = jnp.einsum("rkj,rks->js", folded3, core_time, precision=highest) / math.sqrt(
        total_sensors * total_time
    )
    time_part = jnp.einsum("rkj,rtj->kt", folded3, core_chan, precision=highest) / math.sqrt(
        total_sensors * total_chan
    )
    groups = n_channel * n_time
    share_index = lax.axis_index("channel") * n_time + lax.axis_index("tm")
    share = sensor_rows // groups
    block = edge_weights.shape[-1]
    weights_float = edge_weights.astype(jnp.float32)
    degree = jnp.sum(weights_float, axis=(1, 3)).reshape(sensor_rows)
    reduced = lax.psum_scatter(fit_part, ("channel", "tm"), scatter_dimension=0, tiled=True)
    whole_rows = lax.all_gather(sensor_factor, "sensor", axis=0, tiled=True)
    pulled = pulled_rows(whole_rows, neighbour_ids, weights_float, block).reshape(
        sensor_rows, rank_one
    )
    graph_all = lap_weight * (degree[:, None] * sensor_factor - pulled)
    graph_share = lax.dynamic_slice_in_dim(graph_all, share_index * share, share, 0)
    sensor_grad = reduced + graph_share
    core_grad = lax.psum(core_part, ("sensor", "channel", "tm"))
    channel_grad = lax.psum(chan_part, ("sensor", "tm"))
    time_grad = lax.psum(time_part, ("sensor", "channel"))
    return (core_grad, sensor_grad, channel_grad, time_grad)


def solution(mesh):
    return jax.shard_map(
        on_device,
        mesh=mesh,
        in_specs=(
            P("sensor", "tm", "channel"),
            P(),
            P("sensor", None),
            P("channel", None),
            P("tm", None),
            P("sensor", None),
            P("sensor", None, None, None),
        ),
        out_specs=(P(), P(("sensor", "channel", "tm"), None), P("channel", None), P("tm", None)),
        check_vma=False,
    )
```

profile of v0, /device:TPU:0, one launch (start us, length us, event | category | flops | bytes accessed | tf_op | source)
XLA Modules:
  0.0 556.5 jit_solution(13374377818562630704)
XLA Ops:
  8.0 0.0 copy-start
  8.0 0.0 copy-start.6
  8.0 0.0 reduce-scatter.4.cloned.1.call-start
  8.1 24.9 %copy.27 = f32[768,64,128]{0,2,1:T(8,128)} copy(f32[768,64,128]{2,1,0:T(8,128)} %param.7) | data formatting | bytes 50331648 | tf_op args[0]
  33.0 0.0 copy-done
  33.0 0.0 copy-done.6
  33.0 0.0 copy-start.5
  33.0 1.8 fusion.32
  34.8 0.0 copy-done.5
  34.8 0.0 copy-start.1
  34.8 0.0 copy-start.3
  34.8 1.8 fusion.5
  36.7 0.0 copy-done.1
  36.7 0.0 copy-done.3
  36.7 26.3 %bitcast_subtract_fusion = f32[768,8192]{0,1:T(8,128)} fusion(f32[768,64,128]{0,2,1:T(8,128)} %copy.27, f32[768,64]{0,1:T(8,128)S(1)} %copy-done.3, f32[8,8,64,128]{3,2,1,0:T(8,128)S(1)} %bitcast.77), kind=kOutput, calls=%fused_computation.1 | convolution fusion | flops 4838129664 | bytes 52625408 | tf_op jit(solution)/shard_map/dot_general | solution.py:32
  63.0 20.9 %fusion.14 = f32[768,64]{0,1:T(8,128)S(1)} fusion(f32[768,8192]{0,1:T(8,128)} %bitcast_subtract_fusion, f32[8,8,64,128]{3,2,1,0:T(8,128)S(1)} %bitcast.78), kind=kOutput, calls=%fused_computation.18 | convolution fusion | flops 4831887360 | bytes 27459584 | tf_op jit(solution)/shard_map/dot_general | solution.py:36
  83.8 0.9 copy.34
  84.8 0.0 reduce-scatter.4.cloned.1.call-update
  84.8 0.0 all-gather.2.cloned.1.call-start
  84.8 0.5 all-gather.2.cloned.1.call-update
  85.4 0.0 all-reduce.2.cloned.1.call-start
  85.4 0.0 copy-done.4
  85.4 27.7 %convolution_bitcast_fusion = f32[8,8,64,128]{3,1,2,0:T(8,128)S(1)} fusion(f32[768,8192]{0,1:T(8,128)} %bitcast_subtract_fusion, f32[768,64]{0,1:T(8,128)S(1)} %copy-done.4), kind=kOutput, calls=%fused_computation.12 | convolution fusion | flops 4831838208 | bytes 27459584 | tf_op jit(solution)/shard_map/dot_general | solution.py:35
  113.1 0.4 copy.39
  113.5 1.9 fusion.28
  115.4 2.2 convolution_multiply_fusion
  117.6 0.0 all-reduce.2.cloned.1.call-update
  117.6 5.2 fusion.20
  122.9 0.0 copy-start.7
  122.9 1.9 fusion.26
  124.8 0.0 copy-done.7
  124.8 0.1 copy.28
  124.9 0.1 reshape.31
  125.0 1.6 convert_reduce_fusion
  126.6 129.7 %psum.22 = f32[128,64]{0,1:T(8,128)} all-reduce(f32[128,64]{0,1:T(8,128)S(1)} %fusion.20), channel_id=1, replica_groups=mesh['sensor'=16,'channel'=4,'tm'=2] {'sensor','tm'}, use_global_device_ids=true, to_apply=%region_3.0 | all-reduce | flops 8192 | bytes 65536 | tf_op jit(solution)/shard_map/psum | solution.py:65
  256.3 3.0 fusion.23
  259.3 276.5 %psum.23 = f32[64,32]{0,1:T(8,128)} all-reduce(f32[64,32]{0,1:T(8,128)S(1)} %fusion.23), channel_id=1, replica_groups=mesh['sensor'=16,'channel'=4,'tm'=2] {'sensor','channel'}, use_global_device_ids=true, to_apply=%region_4.0 | all-reduce | flops 2048 | bytes 16384 | tf_op jit(solution)/shard_map/psum | solution.py:66
  535.8 0.1 dynamic-slice
  535.9 0.0 reduce-scatter.4.cloned.1.call-done
  535.9 0.9 copy.35
  536.8 0.0 all-gather.2.cloned.1.call-done
  536.8 4.0 copy_bitcast_fusion
  540.8 0.0 copy-start.2
  540.8 2.6 gather_fusion
  543.4 0.0 copy-done.2
  543.4 1.8 fusion.11
  545.2 1.6 fusion.25
  546.8 2.3 copy.54
  (5 shorter events, 0.0 us)
Async XLA Ops:
  8.0 25.0 %copy-start = (f32[64,64,32]{1,2,0:T(8,128)S(1)}, f32[64,64,32]{1,2,0:T(8,128)}, u32[]{:S(2)}) copy-start(f32[64,64,32]{1,2,0:T(8,128)} %param.8) | copy-start | bytes 1572868
  8.0 24.9 %copy-start.6 = (f32[64,32]{0,1:T(8,128)S(1)}, f32[64,32]{0,1:T(8,128)}, u32[]{:S(2)}) copy-start(f32[64,32]{0,1:T(8,128)} %param.11) | copy-start | bytes 24580
  8.0 527.9 %reduce-scatter.4.cloned.1.call-start = ((), (), s32[]{:S(2)}) async-start(), calls=%async_computation.3 | async-start | bytes 442368
  33.0 1.8 copy-start.5
  34.8 1.9 copy-start.1
  34.8 1.9 copy-start.3
  63.0 22.5 %copy-start.4 = (f32[768,64]{0,1:T(8,128)S(1)}, f32[768,64]{0,1:T(8,128)}, u32[]{:S(2)}) copy-start(f32[768,64]{0,1:T(8,128)} %param.9) | copy-start | bytes 589828
  84.8 452.0 %all-gather.2.cloned.1.call-start = ((), (), s32[]{:S(2)}) async-start(), calls=%async_computation.2 | async-start | bytes 3342336 | tf_op jit(solution)/shard_map/all_gather | solution.py:57
  85.4 461.4 %all-reduce.2.cloned.1.call-start = ((), (), s32[]{:S(2)}) async-start(), calls=%async_computation.1 | async-start | bytes 2097152 | tf_op jit(solution)/shard_map/psum | solution.py:64
  122.9 1.9 copy-start.7
  540.8 2.6 copy-start.2
Sparse Core Ops, SparseCore 0:
  84.9 73.7 reduce-scatter.3
  164.1 146.2 all-reduce.1
Sparse Core Ops, SparseCore 1:
  87.0 38.2 all-gather.1
where the time goes:
time: 557 us; the launch traced here: 556 us
  blocking collectives  406 us (73%)
  matrix products  94.5 us (17%)
  local copies, waits for them, and re-layouts  36.2 us (6%)
  between operations  15.7 us (3%)
    psum x1, blocking collectives, on_device(): time_grad = lax.psum(time_part, ('sensor', 'channel'))  277 us
    psum x1, blocking collectives, on_device(): channel_grad = lax.psum(chan_part, ('sensor', 'tm'))  130 us
    unnamed x21, local copies, waits for them, and re-layouts  29.4 us
    dot_general x1, matrix products, on_device(): folded = jnp.dot(sensor_factor.T, residual, precision=highest)  27.7 us
    dot_general x1, matrix products, on_device(): jnp.dot(sensor_factor, flat_core, precision=highest)  26.3 us
    dot_general x1, matrix products, on_device(): jnp.dot(residual, flat_core.T, precision=highest)  20.9 us
  transfers between devices with their start and end apart: 3, of which 0 were waited for; matrix products, arithmetic and copies ran while one was open for 10% of the time, Pallas kernels for 0%

commit v1 on v0

--- a/solution.py
+++ b/solution.py
@@ -6,6 +6,11 @@
 
 lap_weight = 1.0 / 512.0
 highest = lax.Precision.HIGHEST
+
+
+def gather_and_add(x, mesh_axis):
+    shards = lax.all_gather(x, mesh_axis)
+    return jnp.sum(shards, axis=0)
 
 
 def pulled_rows(whole_factor, neighbour_ids, weights_float, block):
@@ -63,7 +68,7 @@
     sensor_grad = reduced + graph_share
     core_grad = lax.psum(core_part, ("sensor", "channel", "tm"))
     channel_grad = lax.psum(chan_part, ("sensor", "tm"))
-    time_grad = lax.psum(time_part, ("sensor", "channel"))
+    time_grad = gather_and_add(time_part, ("sensor", "channel"))
     return (core_grad, sensor_grad, channel_grad, time_grad)
 
 

time: 557 us -> 425 us (0.76)
  blocking collectives: 406 us -> 273 us
    psum x1 -> x0, blocking collectives: 277 us -> none  [on_device(): time_grad = lax.psum(time_part, ('sensor', 'channel'))]
    all_gather x0 -> x1, blocking collectives: none -> 143 us  [gather_and_add(): shards = lax.all_gather(x, mesh_axis)]
  transfers between devices with their start and end apart: 3 -> 3, of which waited for: 0 -> 0; matrix products, arithmetic and copies ran while one was open for 10% -> 13% of each run, Pallas kernels for 0% -> 0%
where the time goes in v1:
time: 425 us; the launch traced here: 424 us
  blocking collectives  273 us (64%)
  matrix products  94.5 us (22%)
  local copies, waits for them, and re-layouts  36.2 us (9%)
  between operations  15.7 us (4%)
    all_gather x1, blocking collectives, gather_and_add(): shards = lax.all_gather(x, mesh_axis)  143 us
    psum x1, blocking collectives, on_device(): channel_grad = lax.psum(chan_part, ('sensor', 'tm'))  130 us
    unnamed x21, local copies, waits for them, and re-layouts  29.4 us
    dot_general x1, matrix products, on_device(): folded = jnp.dot(sensor_factor.T, residual, precision=highest)  27.7 us
    dot_general x1, matrix products, on_device(): jnp.dot(sensor_factor, flat_core, precision=highest)  26.3 us
    dot_general x1, matrix products, on_device(): jnp.dot(residual, flat_core.T, precision=highest)  20.9 us
  transfers between devices with their start and end apart: 3, of which 0 were waited for; matrix products, arithmetic and copies ran while one was open for 13% of the time, Pallas kernels for 0%

profile of v1, /device:TPU:0, one launch (start us, length us, event | category | flops | bytes accessed | tf_op | source)
XLA Modules:
  0.0 423.7 jit_solution(4798195538514744745)
XLA Ops:
  8.0 0.0 copy-start
  8.0 0.0 copy-start.6
  8.0 0.0 reduce-scatter.4.cloned.1.call-start
  8.1 24.9 %copy.27 = f32[768,64,128]{0,2,1:T(8,128)} copy(f32[768,64,128]{2,1,0:T(8,128)} %param.7) | data formatting | bytes 50331648 | tf_op args[0]
  33.0 0.0 copy-done
  33.0 0.0 copy-done.6
  33.0 0.0 copy-start.5
  33.0 1.8 fusion.33
  34.8 0.0 copy-done.5
  34.8 0.0 copy-start.1
  34.8 0.0 copy-start.3
  34.8 1.8 fusion.5
  36.7 0.0 copy-done.1
  36.7 0.0 copy-done.3
  36.7 26.3 %bitcast_subtract_fusion = f32[768,8192]{0,1:T(8,128)} fusion(f32[768,64,128]{0,2,1:T(8,128)} %copy.27, f32[768,64]{0,1:T(8,128)S(1)} %copy-done.3, f32[8,8,64,128]{3,2,1,0:T(8,128)S(1)} %bitcast.81), kind=kOutput, calls=%fused_computation.1 | convolution fusion | flops 4838129664 | bytes 52625408 | tf_op jit(solution)/shard_map/dot_general | solution.py:37
  63.0 20.9 %fusion.14 = f32[768,64]{0,1:T(8,128)S(1)} fusion(f32[768,8192]{0,1:T(8,128)} %bitcast_subtract_fusion, f32[8,8,64,128]{3,2,1,0:T(8,128)S(1)} %bitcast.82), kind=kOutput, calls=%fused_computation.18 | convolution fusion | flops 4831887360 | bytes 27459584 | tf_op jit(solution)/shard_map/dot_general | solution.py:41
  83.8 0.9 copy.34
  84.8 0.0 reduce-scatter.4.cloned.1.call-update
  84.8 0.0 all-gather.4.cloned.1.call-start
  84.8 0.5 all-gather.4.cloned.1.call-update
  85.4 0.0 all-reduce.2.cloned.1.call-start
  85.4 0.0 copy-done.4
  85.4 27.7 %convolution_bitcast_fusion = f32[8,8,64,128]{3,1,2,0:T(8,128)S(1)} fusion(f32[768,8192]{0,1:T(8,128)} %bitcast_subtract_fusion, f32[768,64]{0,1:T(8,128)S(1)} %copy-done.4), kind=kOutput, calls=%fused_computation.12 | convolution fusion | flops 4831838208 | bytes 27459584 | tf_op jit(solution)/shard_map/dot_general | solution.py:40
  113.1 0.4 copy.39
  113.5 1.9 fusion.29
  115.4 2.2 convolution_multiply_fusion
  117.6 0.0 all-reduce.2.cloned.1.call-update
  117.6 5.2 %fusion.20 = f32[128,64]{0,1:T(8,128)S(1)} fusion(f32[64,64,128]{2,1,0:T(8,128)S(1)} %bitcast.79, f32[64,64,64]{2,0,1:T(8,128)} %copy-done.1), kind=kOutput, calls=%fused_computation.20 | convolution fusion | flops 402661376 | bytes 3178496 | tf_op jit(solution)/shard_map/rkj,rks->js/dot_general | solution.py:49
  122.9 0.0 copy-start.7
  122.9 1.9 fusion.27
  124.8 0.0 copy-done.7
  124.8 0.1 copy.28
  124.9 0.1 reshape.31
  125.0 1.6 convert_reduce_fusion
  126.6 129.7 %psum.15 = f32[128,64]{0,1:T(8,128)} all-reduce(f32[128,64]{0,1:T(8,128)S(1)} %fusion.20), channel_id=1, replica_groups=mesh['sensor'=16,'channel'=4,'tm'=2] {'sensor','tm'}, use_global_device_ids=true, to_apply=%region_3.0 | all-reduce | flops 8192 | bytes 65536 | tf_op jit(solution)/shard_map/psum | solution.py:70
  256.3 3.0 fusion.24
  259.3 143.1 %all-gather.1 = f32[64,64,32]{1,2,0:T(8,128)S(1)} all-gather(f32[1,64,32]{1,2,0:T(8,128)S(1)} %fusion.24), channel_id=2, replica_groups=mesh['sensor'=16,'channel'=4,'tm'=2] {'sensor','channel'}, dimensions={0}, use_global_device_ids=true | all-gather | bytes 532480 | tf_op jit(solution)/shard_map/all_gather | solution.py:12
  402.4 0.1 dynamic-slice
  402.5 0.7 reduce_sum.19
  403.2 0.0 reduce-scatter.4.cloned.1.call-done
  403.2 0.9 copy.35
  404.0 0.0 all-gather.4.cloned.1.call-done
  404.1 4.0 copy_bitcast_fusion
  408.0 2.6 gather_fusion
  410.7 0.0 copy-done.2
  410.7 1.8 fusion.11
  412.5 1.6 fusion.26
  414.0 2.3 copy.54
  (6 shorter events, 0.0 us)
Async XLA Ops:
  8.0 25.0 %copy-start = (f32[64,64,32]{1,2,0:T(8,128)S(1)}, f32[64,64,32]{1,2,0:T(8,128)}, u32[]{:S(2)}) copy-start(f32[64,64,32]{1,2,0:T(8,128)} %param.8) | copy-start | bytes 1572868
  8.0 24.9 %copy-start.6 = (f32[64,32]{0,1:T(8,128)S(1)}, f32[64,32]{0,1:T(8,128)}, u32[]{:S(2)}) copy-start(f32[64,32]{0,1:T(8,128)} %param.11) | copy-start | bytes 24580
  8.0 395.1 %reduce-scatter.4.cloned.1.call-start = ((), (), s32[]{:S(2)}) async-start(), calls=%async_computation.3 | async-start | bytes 442368
  33.0 1.8 copy-start.5
  34.8 1.9 copy-start.1
  34.8 1.9 copy-start.3
  63.0 22.5 %copy-start.4 = (f32[768,64]{0,1:T(8,128)S(1)}, f32[768,64]{0,1:T(8,128)}, u32[]{:S(2)}) copy-start(f32[768,64]{0,1:T(8,128)} %param.9) | copy-start | bytes 589828
  84.8 319.3 %all-gather.4.cloned.1.call-start = ((), (), s32[]{:S(2)}) async-start(), calls=%async_computation.2 | async-start | bytes 3342336 | tf_op jit(solution)/shard_map/all_gather | solution.py:62
  85.4 328.7 %all-reduce.2.cloned.1.call-start = ((), (), s32[]{:S(2)}) async-start(), calls=%async_computation.1 | async-start | bytes 2097152 | tf_op jit(solution)/shard_map/psum | solution.py:69
  122.9 1.9 copy-start.7
  408.0 2.6 copy-start.2
Sparse Core Ops, SparseCore 0:
  84.9 73.7 reduce-scatter.3
  164.1 146.2 all-reduce.1
Sparse Core Ops, SparseCore 1:
  87.0 38.2 all-gather.3

commit v2 on v0

--- a/solution.py
+++ b/solution.py
@@ -63,7 +63,8 @@
     sensor_grad = reduced + graph_share
     core_grad = lax.psum(core_part, ("sensor", "channel", "tm"))
     channel_grad = lax.psum(chan_part, ("sensor", "tm"))
-    time_grad = lax.psum(time_part, ("sensor", "channel"))
+    one_axis = lax.psum(time_part, "sensor")
+    time_grad = lax.psum(one_axis, "channel")
     return (core_grad, sensor_grad, channel_grad, time_grad)
 
 

time: 557 us -> 351 us (0.63)
  blocking collectives: 406 us -> 200 us
    psum x1 -> x2, blocking collectives: 277 us -> 70.4 us  [the longest x1 52.9 us: on_device(): one_axis = lax.psum(time_part, 'sensor')]
  transfers between devices with their start and end apart: 3 -> 3, of which waited for: 0 -> 0; matrix products, arithmetic and copies ran while one was open for 10% -> 16% of each run, Pallas kernels for 0% -> 0%
where the time goes in v2:
time: 351 us; the launch traced here: 350 us
  blocking collectives  200 us (57%)
  matrix products  94.5 us (27%)
  local copies, waits for them, and re-layouts  36.2 us (10%)
  between operations  15.7 us (4%)
    psum x1, blocking collectives, on_device(): channel_grad = lax.psum(chan_part, ('sensor', 'tm'))  130 us
    psum x1, blocking collectives, on_device(): one_axis = lax.psum(time_part, 'sensor')  52.9 us
    unnamed x21, local copies, waits for them, and re-layouts  29.3 us
    dot_general x1, matrix products, on_device(): folded = jnp.dot(sensor_factor.T, residual, precision=highest)  27.7 us
    dot_general x1, matrix products, on_device(): jnp.dot(sensor_factor, flat_core, precision=highest)  26.3 us
    dot_general x1, matrix products, on_device(): jnp.dot(residual, flat_core.T, precision=highest)  20.9 us
    psum x1, blocking collectives, on_device(): time_grad = lax.psum(one_axis, 'channel')  17.5 us
  transfers between devices with their start and end apart: 3, of which 0 were waited for; matrix products, arithmetic and copies ran while one was open for 16% of the time, Pallas kernels for 0%

profile of v2, /device:TPU:0, one launch (start us, length us, event | category | flops | bytes accessed | tf_op | source)
XLA Modules:
  0.0 350.4 jit_solution(4612580875231637469)
XLA Ops:
  8.0 0.0 copy-start
  8.0 0.0 copy-start.6
  8.0 0.0 reduce-scatter.4.cloned.1.call-start
  8.1 24.9 %copy.27 = f32[768,64,128]{0,2,1:T(8,128)} copy(f32[768,64,128]{2,1,0:T(8,128)} %param.7) | data formatting | bytes 50331648 | tf_op args[0]
  32.9 0.0 copy-done
  32.9 0.0 copy-done.6
  32.9 0.0 copy-start.5
  33.0 1.8 fusion.32
  34.8 0.0 copy-done.5
  34.8 0.0 copy-start.1
  34.8 0.0 copy-start.3
  34.8 1.8 fusion.5
  36.7 0.0 copy-done.1
  36.7 0.0 copy-done.3
  36.7 26.3 %bitcast_subtract_fusion = f32[768,8192]{0,1:T(8,128)} fusion(f32[768,64,128]{0,2,1:T(8,128)} %copy.27, f32[768,64]{0,1:T(8,128)S(1)} %copy-done.3, f32[8,8,64,128]{3,2,1,0:T(8,128)S(1)} %bitcast.77), kind=kOutput, calls=%fused_computation.1 | convolution fusion | flops 4838129664 | bytes 52625408 | tf_op jit(solution)/shard_map/dot_general | solution.py:32
  63.0 0.0 copy-start.4
  63.0 20.9 %fusion.14 = f32[768,64]{0,1:T(8,128)S(1)} fusion(f32[768,8192]{0,1:T(8,128)} %bitcast_subtract_fusion, f32[8,8,64,128]{3,2,1,0:T(8,128)S(1)} %bitcast.78), kind=kOutput, calls=%fused_computation.18 | convolution fusion | flops 4831887360 | bytes 27459584 | tf_op jit(solution)/shard_map/dot_general | solution.py:36
  83.8 0.9 copy.34
  84.8 0.0 reduce-scatter.4.cloned.1.call-update
  84.8 0.0 all-gather.2.cloned.1.call-start
  84.8 0.5 all-gather.2.cloned.1.call-update
  85.4 0.0 all-reduce.2.cloned.1.call-start
  85.4 0.0 copy-done.4
  85.4 27.7 %convolution_bitcast_fusion = f32[8,8,64,128]{3,1,2,0:T(8,128)S(1)} fusion(f32[768,8192]{0,1:T(8,128)} %bitcast_subtract_fusion, f32[768,64]{0,1:T(8,128)S(1)} %copy-done.4), kind=kOutput, calls=%fused_computation.12 | convolution fusion | flops 4831838208 | bytes 27459584 | tf_op jit(solution)/shard_map/dot_general | solution.py:35
  113.1 0.4 copy.39
  113.5 1.9 fusion.28
  115.4 2.2 convolution_multiply_fusion
  117.6 0.0 all-reduce.2.cloned.1.call-update
  117.6 5.2 %fusion.20 = f32[128,64]{0,1:T(8,128)S(1)} fusion(f32[64,64,128]{2,1,0:T(8,128)S(1)} %bitcast.75, f32[64,64,64]{2,0,1:T(8,128)} %copy-done.1), kind=kOutput, calls=%fused_computation.20 | convolution fusion | flops 402661376 | bytes 3178496 | tf_op jit(solution)/shard_map/rkj,rks->js/dot_general | solution.py:44
  122.8 0.0 copy-start.7
  122.9 2.0 fusion.26
  124.8 0.0 copy-done.7
  124.8 0.1 copy.28
  124.9 0.1 reshape.31
  125.0 1.6 convert_reduce_fusion
  126.6 129.7 %psum.29 = f32[128,64]{0,1:T(8,128)} all-reduce(f32[128,64]{0,1:T(8,128)S(1)} %fusion.20), channel_id=1, replica_groups=mesh['sensor'=16,'channel'=4,'tm'=2] {'sensor','tm'}, use_global_device_ids=true, to_apply=%region_3.0 | all-reduce | flops 8192 | bytes 65536 | tf_op jit(solution)/shard_map/psum | solution.py:65
  256.3 3.0 fusion.23
  259.3 52.9 %psum.30 = f32[64,32]{0,1:T(8,128)S(1)} all-reduce(f32[64,32]{0,1:T(8,128)S(1)} %fusion.23), channel_id=1, replica_groups=mesh['sensor'=16,'channel'=4,'tm'=2] {'sensor'}, use_global_device_ids=true, to_apply=%region_4.0 | all-reduce | flops 2048 | bytes 16384 | tf_op jit(solution)/shard_map/psum | solution.py:66
  312.2 17.5 %psum.31 = f32[64,32]{0,1:T(8,128)} all-reduce(f32[64,32]{0,1:T(8,128)S(1)} %psum.30), channel_id=1, replica_groups=mesh['sensor'=16,'channel'=4,'tm'=2] {'channel'}, use_global_device_ids=true, to_apply=%region_5.0 | all-reduce | flops 2048 | bytes 16384 | tf_op jit(solution)/shard_map/psum | solution.py:67
  329.7 0.1 dynamic-slice
  329.8 0.9 copy.35
  330.7 0.0 all-gather.2.cloned.1.call-done
  330.7 4.0 %copy_bitcast_fusion = f32[96,128,64]{1,2,0:T(8,128)} fusion(f32[12288,64]{0,1:T(8,128)} %all-gather.2.cloned.1.call-done), kind=kLoop, calls=%fused_computation.2 | loop fusion | bytes 6291456 | tf_op jit(solution)/shard_map/reshape | solution.py:12
  334.7 2.6 gather_fusion
  337.3 0.0 copy-done.2
  337.3 1.8 fusion.11
  339.1 1.6 fusion.25
  340.7 2.3 copy.54
  (6 shorter events, 0.0 us)
Async XLA Ops:
  8.0 24.9 %copy-start = (f32[64,64,32]{1,2,0:T(8,128)S(1)}, f32[64,64,32]{1,2,0:T(8,128)}, u32[]{:S(2)}) copy-start(f32[64,64,32]{1,2,0:T(8,128)} %param.8) | copy-start | bytes 1572868
  8.0 24.9 %copy-start.6 = (f32[64,32]{0,1:T(8,128)S(1)}, f32[64,32]{0,1:T(8,128)}, u32[]{:S(2)}) copy-start(f32[64,32]{0,1:T(8,128)} %param.11) | copy-start | bytes 24580
  8.0 321.8 %reduce-scatter.4.cloned.1.call-start = ((), (), s32[]{:S(2)}) async-start(), calls=%async_computation.3 | async-start | bytes 442368
  32.9 1.9 copy-start.5
  34.8 1.9 copy-start.1
  34.8 1.9 copy-start.3
  63.0 22.5 %copy-start.4 = (f32[768,64]{0,1:T(8,128)S(1)}, f32[768,64]{0,1:T(8,128)}, u32[]{:S(2)}) copy-start(f32[768,64]{0,1:T(8,128)} %param.9) | copy-start | bytes 589828
  84.8 245.9 %all-gather.2.cloned.1.call-start = ((), (), s32[]{:S(2)}) async-start(), calls=%async_computation.2 | async-start | bytes 3342336 | tf_op jit(solution)/shard_map/all_gather | solution.py:57
  85.4 255.3 %all-reduce.2.cloned.1.call-start = ((), (), s32[]{:S(2)}) async-start(), calls=%async_computation.1 | async-start | bytes 2097152 | tf_op jit(solution)/shard_map/psum | solution.py:64
  122.8 2.0 copy-start.7
  334.7 2.6 copy-start.2
Sparse Core Ops, SparseCore 0:
  84.9 73.8 reduce-scatter.3
  164.1 146.0 all-reduce.1
Sparse Core Ops, SparseCore 1:
  87.0 38.2 all-gather.1
